TPU v7x, 256 devices: a whole 4x4x8 slice. The times are simulated.
256 devices in a mesh: wide: 64 (over y, z, core), narrow: 4 (over x).
Axes of the slice: x: 4, y: 4, z: 8, core: 2. Of those that a mesh axis runs over, the one named last changes fastest.
Arguments:
- embedding: float32 [131072, 128], P(('wide', 'narrow'))
- tile_blocks: bfloat16 [64, 4, 22, 512, 512], P('wide', 'narrow'), may hold values from -0.125 to 0.125
- tile_row: int32 [64, 4, 22], P('wide', 'narrow'), may hold values from 0 to 3
- tile_col: int32 [64, 4, 22], P('wide', 'narrow'), may hold values from 0 to 63
- counts: int32 [64, 4], P('wide', 'narrow'), may hold values from 1 to 22, as said below
Outputs:
- orthonormal: float32 [131072, 128], P(('wide', 'narrow'))
Inputs may be any that keep to these rules, and one draw needn't show every extreme that they name: Slots 0 to counts[w, n] - 1 of device (w, n) hold its tiles, the others are unused; some device has all 22 slots live.
All inputs are finite; a program needn't handle non-finite values.
Results may differ from a plain program's by a relative error of at most 0.0036.
Values may be sent and summed in bfloat16 or wider, within the bound.
No kernel may reach another device: no remote copies, remote signals or barrier semaphores. Data moves between devices by JAX's collectives and lax.ppermute only.
A program may use at most 64 MiB of HBM per device.

v0:
```python
import jax
import jax.numpy as jnp
from jax import lax
from jax.sharding import PartitionSpec as P


def apply_operator(values_bf, tile_local, row_local, col_local, live_count):
    tile_size = tile_local.shape[1]
    width = values_bf.shape[1]
    rows_dev = values_bf.shape[0]
    slab_count = lax.axis_size("narrow") * rows_dev // tile_size
    slot_count = tile_local.shape[0]
    gathered = lax.all_gather(values_bf, "wide", axis=0, tiled=True)
    blocks = gathered.reshape(-1, tile_size, width)
    picked = jnp.take(blocks, col_local, axis=0)
    products = jnp.einsum("sij,sjk->sik", tile_local, picked, preferred_element_type=jnp.float32)
    slot_ids = jnp.arange(slot_count, dtype=jnp.int32)
    slab_ids = jnp.arange(slab_count, dtype=jnp.int32)
    onehot = ((row_local[None, :] == slab_ids[:, None]) & (slot_ids[None, :] < live_count)).astype(
        jnp.float32
    )
    partial_value = jnp.einsum("rs,sik->rik", onehot, products, precision=lax.Precision.HIGHEST)
    partial_value = partial_value.reshape(slab_count * tile_size, width)
    slab_total = lax.psum(partial_value, "narrow")
    return lax.dynamic_slice_in_dim(slab_total, lax.axis_index("narrow") * rows_dev, rows_dev, 0)


def local(embedding, tile_blocks, tile_row, tile_col, counts):
    tile_local = tile_blocks[0, 0]
    row_local = tile_row[0, 0]
    col_local = tile_col[0, 0]
    live_count = counts[0, 0]
    emb_bf = embedding.astype(jnp.bfloat16)
    first_order = apply_operator(emb_bf, tile_local, row_local, col_local, live_count)
    first_bf = first_order.astype(jnp.bfloat16)
    second = (
        2.0 * apply_operator(first_bf, tile_local, row_local, col_local, live_count) - embedding
    )
    spectral = 1.2661 * embedding - 1.1303 * first_order + 0.2715 * second
    gram_part = lax.dot_general(
        spectral, spectral, (((0,), (0,)), ((), ())), precision=lax.Precision.HIGHEST
    )
    gram_matrix = lax.psum(gram_part, ("wide", "narrow"))
    lower_factor = jnp.linalg.cholesky(gram_matrix)
    solved = jax.scipy.linalg.solve_triangular(lower_factor, spectral.T, lower=True)
    node_total = embedding.shape[0] * lax.axis_size("wide") * lax.axis_size("narrow")
    return solved.T * jnp.sqrt(jnp.float32(node_total))


def solution(mesh):
    placed = (
        P(("wide", "narrow"), None),
        P("wide", "narrow", None, None, None),
        P("wide", "narrow", None),
        P("wide", "narrow", None),
        P("wide", "narrow"),
    )
    return jax.shard_map(
        local, mesh=mesh, in_specs=placed, out_specs=P(("wide", "narrow"), None), check_vma=False
    )
```

profile of v0, /device:TPU:1, one launch (start us, length us, event | category | flops | bytes accessed | tf_op | source)
XLA Modules:
  0.0 617.0 jit_solution(5770539556316250015)
XLA Ops:
  6.5 0.0 all-gather.3.cloned.1.call-start
  6.5 1.6 convert_element_type.8
  8.2 0.0 all-gather.3.cloned.1.call-update
  8.2 0.0 all-reduce.4.cloned.1.call-start
  8.9 0.7 compare_select_fusion
  9.6 0.7 compare_and_fusion
  10.2 87.1 %all-gather.3.cloned.1.call-done = bf16[32768,128]{1,0:T(8,128)(2,1)} async-done(((bf16[512,128]{1,0:T(8,128)(2,1)}), bf16[32768,128]{1,0:T(8,128)(2,1)}) %all-gather.3.cloned.1.call-update) | async-done | bytes 8388624 | tf_op jit(solution)/shard_map/all_gather | solution.py:13
  97.3 4.5 gather_fusion
  101.8 11.3 %fusion.2 = f32[22,128,512]{2,1,0:T(8,128)} fusion(bf16[1,1,22,512,512]{4,3,2,1,0:T(8,128)(2,1)} %param.8, bf16[22,512,128]{2,1,0:T(8,128)(2,1)S(1)} %gather_fusion, pred[22]{0:T(512)(128)(4,1)S(1)} %compare_and_fusion), kind=kOutput, calls=%fused_computation.4 | convolution fusion | flops 1477836800 | bytes 20185110 | tf_op jit(solution)/shard_map/sij,sjk->sik/dot_general | solution.py:16
  113.1 0.0 copy-start.1
  113.1 6.5 %copy.12 = f32[22,128,512]{1,0,2:T(8,128)} copy(f32[22,128,512]{2,1,0:T(8,128)} %fusion.2) | data formatting | bytes 11534336 | tf_op jit(solution)/shard_map/sij,sjk->sik/dot_general | solution.py:16
  119.6 0.0 copy-done.1
  119.6 5.0 fusion.6
  124.6 1.0 copy.8
  125.6 0.0 all-reduce.4.cloned.1.call-update
  125.6 0.0 all-gather.5.cloned.1.call-start
  125.7 45.8 %all-reduce.4.cloned.1.call-done = f32[2048,128]{1,0:T(8,128)} async-done(((f32[2048,128]{1,0:T(8,128)}), f32[2048,128]{1,0:T(8,128)}) %all-reduce.4.cloned.1.call-update) | async-done | bytes 1048592 | tf_op jit(solution)/shard_map/psum | solution.py:24
  171.5 1.6 dynamic-slice_convert_fusion
  173.2 0.0 all-gather.5.cloned.1.call-update
  173.2 0.2 all-reduce.6.cloned.1.call-start
  173.4 87.1 %all-gather.5.cloned.1.call-done = bf16[32768,128]{1,0:T(8,128)(2,1)} async-done(((bf16[512,128]{1,0:T(8,128)(2,1)}), bf16[32768,128]{1,0:T(8,128)(2,1)}) %all-gather.5.cloned.1.call-update) | async-done | bytes 8388624 | tf_op jit(solution)/shard_map/all_gather | solution.py:13
  260.5 4.5 gather_fusion.1
  265.0 11.3 %fusion = f32[22,128,512]{2,1,0:T(8,128)} fusion(bf16[1,1,22,512,512]{4,3,2,1,0:T(8,128)(2,1)} %param.8, bf16[22,512,128]{2,1,0:T(8,128)(2,1)S(1)} %gather_fusion.1, pred[22]{0:T(512)(128)(4,1)S(1)} %compare_and_fusion), kind=kOutput, calls=%fused_computation.2 | convolution fusion | flops 1477836800 | bytes 20185110 | tf_op jit(solution)/shard_map/sij,sjk->sik/dot_general | solution.py:16
  276.3 6.4 %copy.13 = f32[22,128,512]{1,0,2:T(8,128)} copy(f32[22,128,512]{2,1,0:T(8,128)} %fusion) | data formatting | bytes 11534336 | tf_op jit(solution)/shard_map/sij,sjk->sik/dot_general | solution.py:16
  282.7 0.0 copy-start
  282.7 5.1 fusion.4
  287.8 1.1 copy.9
  288.9 0.0 all-reduce.6.cloned.1.call-update
  288.9 0.3 all-reduce.8.cloned.1.call-start
  289.2 45.6 %all-reduce.6.cloned.1.call-done = f32[2048,128]{1,0:T(8,128)} async-done(((f32[2048,128]{1,0:T(8,128)}), f32[2048,128]{1,0:T(8,128)}) %all-reduce.6.cloned.1.call-update) | async-done | bytes 1048592 | tf_op jit(solution)/shard_map/psum | solution.py:24
  334.8 0.0 copy-done
  334.8 1.1 multiply_add_fusion
  335.9 1.2 fusion.23
  337.1 0.0 all-reduce.8.cloned.1.call-update
  337.1 247.6 %all-reduce.8.cloned.1.call-done = f32[128,128]{0,1:T(8,128)} async-done(((f32[128,128]{0,1:T(8,128)}), f32[128,128]{0,1:T(8,128)}) %all-reduce.8.cloned.1.call-update) | async-done | bytes 65552 | tf_op jit(solution)/shard_map/psum | solution.py:43
  584.7 0.9 copy.11
  585.6 0.9 fusion.16
  586.5 11.7 %cholesky.16 = f32[128,128]{1,0:T(8,128)S(1)} custom-call(f32[128,128]{1,0:T(8,128)S(1)} %fusion.16), custom_call_target="Cholesky" | custom-call | tf_op jit(solution)/shard_map/jit(cholesky)/cholesky | solution.py:44
  598.2 0.6 compare_reduce_fusion
  598.9 0.7 fusion.14
  599.5 9.8 %custom-call.7 = f32[1,128,128]{1,2,0:T(8,128)S(1)} custom-call(f32[1,128,128]{2,1,0:T(8,128)S(1)} %fusion.14), custom_call_target="InvertDiagBlocksLowerTriangular" | custom-call | tf_op jit(solution)/shard_map/jit(_solve_triangular)/triangular_solve | solution.py:45
  609.4 1.1 convolution_multiply_fusion
  (3 shorter events, 0.1 us)
Async XLA Ops:
  6.5 90.8 %all-gather.3.cloned.1.call-start = ((), (), s32[]{:S(2)}) async-start(), calls=%async_computation | async-start | bytes 8519680 | tf_op jit(solution)/shard_map/all_gather | solution.py:13
  8.2 163.4 %all-reduce.4.cloned.1.call-start = ((), (), s32[]{:S(2)}) async-start(), calls=%async_computation.1 | async-start | bytes 2097152 | tf_op jit(solution)/shard_map/psum | solution.py:24
  113.1 6.5 %copy-start.1 = (s32[1,1,22]{2,1,0:T(1,128)S(1)}, s32[1,1,22]{2,1,0:T(1,128)}, u32[]{:S(2)}) copy-start(s32[1,1,22]{2,1,0:T(1,128)} %param.9) | copy-start | bytes 268
  125.6 134.9 %all-gather.5.cloned.1.call-start = ((), (), s32[]{:S(2)}) async-start(), calls=%async_computation.2 | async-start | bytes 8519680 | tf_op jit(solution)/shard_map/all_gather | solution.py:13
  173.2 161.6 %all-reduce.6.cloned.1.call-start = ((), (), s32[]{:S(2)}) async-start(), calls=%async_computation.3 | async-start | bytes 2097152 | tf_op jit(solution)/shard_map/psum | solution.py:24
  282.7 52.1 %copy-start = (f32[512,128]{1,0:T(8,128)S(1)}, f32[512,128]{1,0:T(8,128)}, u32[]{:S(2)}) copy-start(f32[512,128]{1,0:T(8,128)} %param.7) | copy-start | bytes 786436
  288.9 295.8 %all-reduce.8.cloned.1.call-start = ((), (), s32[]{:S(2)}) async-start(), calls=%async_computation.4 | async-start | bytes 131072 | tf_op jit(solution)/shard_map/psum | solution.py:43
Sparse Core Ops, SparseCore 0:
  10.1 87.1 all-gather.2
  125.8 45.7 all-reduce.3
  174.3 86.1 all-gather.4
  289.0 45.7 all-reduce.5
  340.1 244.5 all-reduce.7
where the time goes:
time: 618 us; the launch traced here: 617 us
  waiting for transfers between devices  513 us (83%)
  matrix products  34.9 us (6%)
  other arithmetic  27.8 us (4%)
  local copies, waits for them, and re-layouts  26.5 us (4%)
  between operations  13.9 us (2%)
    psum x1, waiting for transfers between devices, local(): gram_matrix = lax.psum(gram_part, ('wide', 'narrow'))  248 us
    all_gather x2, waiting for transfers between devices, apply_operator(): gathered = lax.all_gather(values_bf, 'wide', axis=0, tiled=True)  174 us
    psum x2, waiting for transfers between devices, apply_operator(): slab_total = lax.psum(partial_value, 'narrow')  91.4 us
    dot_general x2, matrix products, apply_operator(): jnp.einsum('sij,sjk->sik', tile_local, picked, preferred_element_type=jnp...  22.5 us
    dot_general x2, local copies, waits for them, and re-layouts, apply_operator(): jnp.einsum('sij,sjk->sik', tile_local, picked, preferred_element_type=jnp...  12.9 us
    another operation x3, other arithmetic, local(): lower_factor = jnp.linalg.cholesky(gram_matrix)  12.4 us
  transfers between devices with their start and end apart: 5, of which 5 were waited for; matrix products, arithmetic and copies ran while one was open for 0% of the time, Pallas kernels for 0%

commit v1 on v0

--- a/solution.py
+++ b/solution.py
@@ -1,7 +1,18 @@
+import functools
 import jax
 import jax.numpy as jnp
 from jax import lax
 from jax.sharding import PartitionSpec as P
+from jax.lax import psum
+
+
+def note_column_over_axis(content, dev_axis, comm_axis):
+    for j in (dev_axis, comm_axis):
+        content = psum(content, axis_name=j)
+    return content
+
+
+close_stages_all_on = functools.partial(note_column_over_axis, dev_axis="wide", comm_axis="narrow")
 
 
 def apply_operator(values_bf, tile_local, row_local, col_local, live_count):
@@ -40,7 +51,7 @@
     gram_part = lax.dot_general(
         spectral, spectral, (((0,), (0,)), ((), ())), precision=lax.Precision.HIGHEST
     )
-    gram_matrix = lax.psum(gram_part, ("wide", "narrow"))
+    gram_matrix = close_stages_all_on(gram_part)
     lower_factor = jnp.linalg.cholesky(gram_matrix)
     solved = jax.scipy.linalg.solve_triangular(lower_factor, spectral.T, lower=True)
     node_total = embedding.shape[0] * lax.axis_size("wide") * lax.axis_size("narrow")

time: 618 us -> 589 us (0.953)
  waiting for transfers between devices: 513 us -> 483 us
    psum x1 -> x2, waiting for transfers between devices: 248 us -> 217 us  [note_column_over_axis(): content = psum(content, axis_name=j)]
  transfers between devices with their start and end apart: 5 -> 6, of which waited for: 5 -> 6; matrix products, arithmetic and copies ran while one was open for 0% -> 0% of each run, Pallas kernels for 0% -> 0%
where the time goes in v1:
time: 589 us; the launch traced here: 587 us
  waiting for transfers between devices  483 us (82%)
  matrix products  34.9 us (6%)
  other arithmetic  27.8 us (5%)
  local copies, waits for them, and re-layouts  26.5 us (4%)
  between operations  14.2 us (2%)
    psum x2, waiting for transfers between devices, note_column_over_axis(): content = psum(content, axis_name=j)  217 us
    all_gather x2, waiting for transfers between devices, apply_operator(): gathered = lax.all_gather(values_bf, 'wide', axis=0, tiled=True)  174 us
    psum x2, waiting for transfers between devices, apply_operator(): slab_total = lax.psum(partial_value, 'narrow')  91.7 us
    dot_general x2, matrix products, apply_operator(): jnp.einsum('sij,sjk->sik', tile_local, picked, preferred_element_type=jnp...  22.5 us
    dot_general x2, local copies, waits for them, and re-layouts, apply_operator(): jnp.einsum('sij,sjk->sik', tile_local, picked, preferred_element_type=jnp...  12.9 us
    another operation x3, other arithmetic, local(): lower_factor = jnp.linalg.cholesky(gram_matrix)  12.4 us
  transfers between devices with their start and end apart: 6, of which 6 were waited for; matrix products, arithmetic and copies ran while one was open for 0% of the time, Pallas kernels for 0%

profile of v1, /device:TPU:1, one launch (start us, length us, event | category | flops | bytes accessed | tf_op | source)
XLA Modules:
  0.0 587.5 jit_solution(11351835693604825393)
XLA Ops:
  6.5 0.0 all-gather.3.cloned.1.call-start
  6.5 1.6 convert_element_type.8
  8.2 0.0 all-gather.3.cloned.1.call-update
  8.2 0.0 all-reduce.5.cloned.1.call-start
  8.9 0.7 compare_select_fusion
  9.6 0.7 compare_and_fusion
  10.2 87.1 %all-gather.3.cloned.1.call-done = bf16[32768,128]{1,0:T(8,128)(2,1)} async-done(((bf16[512,128]{1,0:T(8,128)(2,1)}), bf16[32768,128]{1,0:T(8,128)(2,1)}) %all-gather.3.cloned.1.call-update) | async-done | bytes 8388624 | tf_op jit(solution)/shard_map/all_gather | solution.py:24
  97.3 4.5 gather_fusion
  101.8 11.3 %fusion.2 = f32[22,128,512]{2,1,0:T(8,128)} fusion(bf16[1,1,22,512,512]{4,3,2,1,0:T(8,128)(2,1)} %param.8, bf16[22,512,128]{2,1,0:T(8,128)(2,1)S(1)} %gather_fusion, pred[22]{0:T(512)(128)(4,1)S(1)} %compare_and_fusion), kind=kOutput, calls=%fused_computation.4 | convolution fusion | flops 1477836800 | bytes 20185110 | tf_op jit(solution)/shard_map/sij,sjk->sik/dot_general | solution.py:27
  113.1 0.0 copy-start.1
  113.1 6.5 %copy.12 = f32[22,128,512]{1,0,2:T(8,128)} copy(f32[22,128,512]{2,1,0:T(8,128)} %fusion.2) | data formatting | bytes 11534336 | tf_op jit(solution)/shard_map/sij,sjk->sik/dot_general | solution.py:27
  119.6 0.0 copy-done.1
  119.6 5.0 fusion.6
  124.6 1.0 copy.8
  125.6 0.0 all-reduce.5.cloned.1.call-update
  125.6 0.0 all-gather.5.cloned.1.call-start
  125.7 45.8 %all-reduce.5.cloned.1.call-done = f32[2048,128]{1,0:T(8,128)} async-done(((f32[2048,128]{1,0:T(8,128)}), f32[2048,128]{1,0:T(8,128)}) %all-reduce.5.cloned.1.call-update) | async-done | bytes 1048592 | tf_op jit(solution)/shard_map/psum | solution.py:35
  171.5 1.6 dynamic-slice_convert_fusion
  173.2 0.0 all-gather.5.cloned.1.call-update
  173.2 0.2 all-reduce.7.cloned.1.call-start
  173.4 87.1 %all-gather.5.cloned.1.call-done = bf16[32768,128]{1,0:T(8,128)(2,1)} async-done(((bf16[512,128]{1,0:T(8,128)(2,1)}), bf16[32768,128]{1,0:T(8,128)(2,1)}) %all-gather.5.cloned.1.call-update) | async-done | bytes 8388624 | tf_op jit(solution)/shard_map/all_gather | solution.py:24
  260.5 4.5 gather_fusion.1
  265.0 11.3 %fusion = f32[22,128,512]{2,1,0:T(8,128)} fusion(bf16[1,1,22,512,512]{4,3,2,1,0:T(8,128)(2,1)} %param.8, bf16[22,512,128]{2,1,0:T(8,128)(2,1)S(1)} %gather_fusion.1, pred[22]{0:T(512)(128)(4,1)S(1)} %compare_and_fusion), kind=kOutput, calls=%fused_computation.2 | convolution fusion | flops 1477836800 | bytes 20185110 | tf_op jit(solution)/shard_map/sij,sjk->sik/dot_general | solution.py:27
  276.3 6.4 %copy.13 = f32[22,128,512]{1,0,2:T(8,128)} copy(f32[22,128,512]{2,1,0:T(8,128)} %fusion) | data formatting | bytes 11534336 | tf_op jit(solution)/shard_map/sij,sjk->sik/dot_general | solution.py:27
  282.7 0.0 copy-start
  282.7 5.1 fusion.4
  287.8 1.1 copy.9
  288.9 0.0 all-reduce.7.cloned.1.call-update
  288.9 0.0 all-reduce.9.cloned.1.call-start
  289.0 45.8 %all-reduce.7.cloned.1.call-done = f32[2048,128]{1,0:T(8,128)} async-done(((f32[2048,128]{1,0:T(8,128)}), f32[2048,128]{1,0:T(8,128)}) %all-reduce.7.cloned.1.call-update) | async-done | bytes 1048592 | tf_op jit(solution)/shard_map/psum | solution.py:35
  334.8 0.0 copy-done
  334.8 1.1 multiply_add_fusion
  335.9 1.2 fusion.23
  337.1 0.0 all-reduce.9.cloned.1.call-update
  337.1 0.3 all-reduce.11.cloned.1.call-start
  337.4 174.4 %all-reduce.9.cloned.1.call-done = f32[128,128]{0,1:T(8,128)} async-done(((f32[128,128]{0,1:T(8,128)}), f32[128,128]{0,1:T(8,128)}) %all-reduce.9.cloned.1.call-update) | async-done | bytes 65552 | tf_op jit(solution)/shard_map/psum | solution.py:11
  511.8 0.0 all-reduce.11.cloned.1.call-update
  511.8 43.1 %all-reduce.11.cloned.1.call-done = f32[128,128]{0,1:T(8,128)} async-done(((f32[128,128]{0,1:T(8,128)}), f32[128,128]{0,1:T(8,128)}) %all-reduce.11.cloned.1.call-update) | async-done | bytes 65552 | tf_op jit(solution)/shard_map/psum | solution.py:11
  554.9 0.9 copy.11
  555.8 0.9 fusion.16
  556.7 11.7 %cholesky.16 = f32[128,128]{1,0:T(8,128)S(1)} custom-call(f32[128,128]{1,0:T(8,128)S(1)} %fusion.16), custom_call_target="Cholesky" | custom-call | tf_op jit(solution)/shard_map/jit(cholesky)/cholesky | solution.py:55
  568.5 0.6 compare_reduce_fusion
  569.1 0.7 fusion.14
  569.8 9.8 %custom-call.7 = f32[1,128,128]{1,2,0:T(8,128)S(1)} custom-call(f32[1,128,128]{2,1,0:T(8,128)S(1)} %fusion.14), custom_call_target="InvertDiagBlocksLowerTriangular" | custom-call | tf_op jit(solution)/shard_map/jit(_solve_triangular)/triangular_solve | solution.py:56
  579.6 1.1 convolution_multiply_fusion
  (3 shorter events, 0.1 us)
Async XLA Ops:
  6.5 90.8 %all-gather.3.cloned.1.call-start = ((), (), s32[]{:S(2)}) async-start(), calls=%async_computation | async-start | bytes 8519680 | tf_op jit(solution)/shard_map/all_gather | solution.py:24
  8.2 163.4 %all-reduce.5.cloned.1.call-start = ((), (), s32[]{:S(2)}) async-start(), calls=%async_computation.1 | async-start | bytes 2097152 | tf_op jit(solution)/shard_map/psum | solution.py:35
  113.1 6.5 %copy-start.1 = (s32[1,1,22]{2,1,0:T(1,128)S(1)}, s32[1,1,22]{2,1,0:T(1,128)}, u32[]{:S(2)}) copy-start(s32[1,1,22]{2,1,0:T(1,128)} %param.9) | copy-start | bytes 268
  125.6 134.9 %all-gather.5.cloned.1.call-start = ((), (), s32[]{:S(2)}) async-start(), calls=%async_computation.2 | async-start | bytes 8519680 | tf_op jit(solution)/shard_map/all_gather | solution.py:24
  173.2 161.6 %all-reduce.7.cloned.1.call-start = ((), (), s32[]{:S(2)}) async-start(), calls=%async_computation.3 | async-start | bytes 2097152 | tf_op jit(solution)/shard_map/psum | solution.py:35
  282.7 52.1 %copy-start = (f32[512,128]{1,0:T(8,128)S(1)}, f32[512,128]{1,0:T(8,128)}, u32[]{:S(2)}) copy-start(f32[512,128]{1,0:T(8,128)} %param.7) | copy-start | bytes 786436
  288.9 222.9 %all-reduce.9.cloned.1.call-start = ((), (), s32[]{:S(2)}) async-start(), calls=%async_computation.4 | async-start | bytes 131072 | tf_op jit(solution)/shard_map/psum | solution.py:11
  337.1 217.8 %all-reduce.11.cloned.1.call-start = ((), (), s32[]{:S(2)}) async-start(), calls=%async_computation.5 | async-start | bytes 131072 | tf_op jit(solution)/shard_map/psum | solution.py:11
Sparse Core Ops, SparseCore 0:
  10.1 87.1 all-gather.2
  125.8 45.7 all-reduce.4
  174.3 86.1 all-gather.4
  289.0 45.7 all-reduce.6
  338.1 173.6 all-reduce.8
  514.0 40.8 all-reduce.10
